TPU v7x, 256 devices: a whole 4x4x8 slice. The times are simulated.
256 devices in a mesh: mom: 32 (over x, z), tm: 8 (over y, core).
Axes of the slice: x: 4, y: 4, z: 8, core: 2. Of those that a mesh axis runs over, the one named last changes fastest.
Arguments:
- green: bfloat16 [64, 32, 128, 2048], P('mom', None, None, 'tm'), may hold values from -6 to 6
- hole: bfloat16 [64, 32, 128, 2048], P('mom', None, None, 'tm'), may hold values from -6 to 6
- decay_log: float32 [64, 8, 2048], P('mom', None, 'tm'), as said below
- phase_step: float32 [64, 8, 2048], P('mom', None, 'tm'), may hold values from -1 to 1
Outputs:
- collision: bfloat16 [64, 32, 128, 2048], P('mom', None, None, 'tm')
Inputs may be any that keep to these rules, and one draw needn't show every extreme that they name: decay_log holds logarithms of decay factors of at most one.
All inputs are finite; a program needn't handle non-finite values.
Results may differ from a plain program's by a relative error of at most 0.0067.
Values may be sent and summed in bfloat16 or wider, within the bound.
A program may use at most 128 MiB of HBM per device.

v0:
```python
import math

import jax
import jax.numpy as jnp
from jax import lax
from jax.sharding import PartitionSpec as P

MOMENTA = 64
ORBITALS = 8


step_weight = 0.0625
coupling = 0.25
exact = lax.Precision.HIGHEST


def prefix(x, axis, combine, identity):
    devices, here = (lax.axis_size(axis), lax.axis_index(axis))
    everything = jax.tree.map(lambda part: lax.all_gather(part, axis), x)
    start = jax.tree.map(
        lambda part, zero: jnp.broadcast_to(jnp.asarray(zero, part.dtype), part.shape), x, identity
    )

    def turn(k, before):
        reached = k < here
        new = combine(before, jax.tree.map(lambda part: part[k], everything))
        return jax.tree.map(lambda a, b: jnp.where(reached, a, b), new, before)

    return lax.fori_loop(0, devices, turn, start)


def transform_matrix(handed):
    numbers = jnp.arange(MOMENTA, dtype=jnp.int32)
    product = numbers[:, None] * numbers[None, :] % MOMENTA
    angles = product.astype(jnp.float32) * (2.0 * math.pi / MOMENTA)
    scaled = 1.0 / math.sqrt(MOMENTA)
    cosine = (jnp.cos(angles) * scaled).astype(jnp.bfloat16)
    sine = (handed * jnp.sin(angles) * scaled).astype(jnp.bfloat16)
    upper = jnp.stack([cosine, -sine], axis=-1)
    lower = jnp.stack([sine, cosine], axis=-1)
    return jnp.stack([upper, lower], axis=1)


def transform(matrix, field):
    return jnp.einsum("rokI,kRpIC->rRpoC", matrix, field, preferred_element_type=jnp.float32)


def self_energy(green_space, hole_space):
    green_re = green_space[:, :, :, 0, :]
    green_im = green_space[:, :, :, 1, :]
    hole_re = hole_space[:, :, :, 0, :]
    hole_im = hole_space[:, :, :, 1, :]
    square_re = green_re * green_re - green_im * green_im
    square_im = 2.0 * green_re * green_im
    energy_re = coupling * (square_re * hole_re - square_im * hole_im)
    energy_im = coupling * (square_re * hole_im + square_im * hole_re)
    return jnp.stack([energy_re, energy_im], axis=3).astype(jnp.bfloat16)


def momentum_energy(pieces, plus, minus):
    green_part, hole_part = pieces
    momenta, row_count, field_width, columns = green_part.shape
    layout = (momenta, row_count, field_width // 2, 2, columns)
    green_space = transform(plus, green_part.reshape(layout))
    hole_space = transform(minus, hole_part.reshape(layout))
    sigma_space = self_energy(green_space, hole_space)
    return transform(minus, sigma_space)


def chain_step(earlier, later):
    early_re, early_im, early_hre, early_him = earlier
    later_re, later_im, later_hre, later_him = later
    wide_re = later_re[:, None, None, :]
    wide_im = later_im[:, None, None, :]
    return (
        early_re * later_re - early_im * later_im,
        early_re * later_im + early_im * later_re,
        wide_re * early_hre - wide_im * early_him + later_hre,
        wide_re * early_him + wide_im * early_hre + later_him,
    )


def apply_kernel(signal, kernel):
    return jnp.einsum(
        "kRabs,kbsu->kRabu", signal, kernel, precision=exact, preferred_element_type=jnp.float32
    )


def block_history(packed):
    signal, levels, phases = packed
    columns = signal.shape[-1]
    source_index = lax.broadcasted_iota(jnp.int32, (columns, columns), 0)
    target_index = lax.broadcasted_iota(jnp.int32, (columns, columns), 1)
    causal = target_index >= source_index
    spread = levels[..., None, :] - levels[..., :, None]
    magnitude = jnp.exp(jnp.where(causal, spread, -10000.0))
    twist = phases[..., None, :] - phases[..., :, None]
    kernel_re = magnitude * jnp.cos(twist)
    kernel_im = magnitude * jnp.sin(twist)
    signal_re = signal[..., 0, :]
    signal_im = signal[..., 1, :]
    out_re = apply_kernel(signal_re, kernel_re) - apply_kernel(signal_im, kernel_im)
    out_im = apply_kernel(signal_re, kernel_im) + apply_kernel(signal_im, kernel_re)
    return jnp.stack([out_re, out_im], axis=-2)


def collide(signal, decay_rows, phase_rows):
    momenta = signal.shape[0]
    levels = jnp.cumsum(decay_rows, axis=-1)
    phases = jnp.cumsum(phase_rows, axis=-1)
    blocked = (
        signal.reshape((momenta // momenta, momenta) + signal.shape[1:]),
        levels.reshape((momenta // momenta, momenta) + levels.shape[1:]),
        phases.reshape((momenta // momenta, momenta) + phases.shape[1:]),
    )
    local = lax.map(block_history, blocked).reshape(signal.shape)
    closing = jnp.exp(levels[..., -1])
    product_re = closing * jnp.cos(phases[..., -1])
    product_im = closing * jnp.sin(phases[..., -1])
    ending_re = local[..., 0, -1]
    ending_im = local[..., 1, -1]
    identity = (
        jnp.ones_like(product_re),
        jnp.zeros_like(product_im),
        jnp.zeros_like(ending_re),
        jnp.zeros_like(ending_im),
    )
    incoming = prefix((product_re, product_im, ending_re, ending_im), "tm", chain_step, identity)
    growth = jnp.exp(levels)
    grow_re = (growth * jnp.cos(phases))[:, None, None, :, :]
    grow_im = (growth * jnp.sin(phases))[:, None, None, :, :]
    enter_re = incoming[2][..., None]
    enter_im = incoming[3][..., None]
    added_re = grow_re * enter_re - grow_im * enter_im
    added_im = grow_re * enter_im + grow_im * enter_re
    return step_weight * (local + jnp.stack([added_re, added_im], axis=-2))


def shards(green, hole, decay_log, phase_step):
    plus = transform_matrix(1.0)
    minus = transform_matrix(-1.0)
    energy = momentum_energy(
        (
            lax.all_to_all(green, "mom", split_axis=2, concat_axis=0, tiled=True),
            lax.all_to_all(hole, "mom", split_axis=2, concat_axis=0, tiled=True),
        ),
        plus,
        minus,
    )
    momenta, row_count, pair_width, two_parts, columns = energy.shape
    flat = energy.reshape(momenta, row_count, pair_width * two_parts, columns)
    returned = lax.all_to_all(flat, "mom", split_axis=0, concat_axis=2, tiled=True)
    momenta, row_count, field_width, columns = returned.shape
    grouped = returned.reshape(momenta, row_count, ORBITALS, ORBITALS, 2, columns)
    result = collide(grouped, decay_log, phase_step)
    return result.reshape(momenta, row_count, field_width, columns).astype(jnp.bfloat16)


def solution(mesh):
    in_specs = (
        P("mom", None, None, "tm"),
        P("mom", None, None, "tm"),
        P("mom", None, "tm"),
        P("mom", None, "tm"),
    )
    out_specs = P("mom", None, None, "tm")
    return jax.shard_map(shards, mesh=mesh, in_specs=in_specs, out_specs=out_specs, check_vma=False)
```

profile of v0, /device:TPU:33, one launch (start us, length us, event | category | flops | bytes accessed | tf_op | source)
XLA Modules:
  0.0 589.1 jit_solution(10592652045339290652)
XLA Ops:
  0.0 6.6 %copy.61 = bf16[2,32,128,256]{3,1,0,2:T(8,128)(2,1)} copy(bf16[2,32,128,256]{3,2,1,0:T(8,128)(2,1)} %param.7) | data formatting | bytes 8388608 | tf_op args[1]
  6.6 10.7 %all-to-all-start.1 = ((bf16[2,32,128,256]{3,1,0,2:T(8,128)(2,1)}), bf16[2,32,128,256]{3,1,0,2:T(8,128)(2,1)}, u32[]{:S(2)}, u32[]{:S(2)}) async-start(bf16[2,32,128,256]{3,1,0,2:T(8,128)(2,1)} %copy.61), calls=%async_computation.1 | async-start | bytes 8388608 | tf_op jit(solution)/shard_map/all_to_all | solution.py:145
  17.3 6.5 %copy.59 = bf16[2,32,128,256]{3,1,0,2:T(8,128)(2,1)} copy(bf16[2,32,128,256]{3,2,1,0:T(8,128)(2,1)} %param.6) | data formatting | bytes 8388608 | tf_op args[0]
  23.8 89.5 %all-to-all-done.1 = bf16[2,32,128,256]{3,1,0,2:T(8,128)(2,1)} async-done(((bf16[2,32,128,256]{3,1,0,2:T(8,128)(2,1)}), bf16[2,32,128,256]{3,1,0,2:T(8,128)(2,1)}, u32[]{:S(2)}, u32[]{:S(2)}) %all-to-all-start.1) | async-done | bytes 4194336 | tf_op jit(solution)/shard_map/all_to_all | solution.py:145
  113.3 6.6 %all-to-all-start = ((bf16[2,32,128,256]{3,1,0,2:T(8,128)(2,1)}), bf16[2,32,128,256]{3,1,0,2:T(8,128)(2,1)}, u32[]{:S(2)}, u32[]{:S(2)}) async-start(bf16[2,32,128,256]{3,1,0,2:T(8,128)(2,1)} %copy.59), calls=%async_computation | async-start | bytes 8388608 | tf_op jit(solution)/shard_map/all_to_all | solution.py:144
  119.9 0.1 multiply_convert_fusion.4
  120.1 0.1 multiply_convert_fusion.2
  120.2 0.1 fusion.61
  120.4 8.5 %copy.107 = bf16[2,32,32,4,256]{4,0,2,3,1:T(2,128)(2,1)} copy(bf16[2,32,32,4,256]{4,1,0,3,2:T(8,128)(2,1)} %bitcast.20) | data formatting | bytes 8388608 | tf_op jit(solution)/shard_map/all_to_all | solution.py:145
  128.9 7.2 %reshape.326 = bf16[64,32,2,2,256,1]{4,0,3,2,1,5:T(8,128)(2,1)} reshape(bf16[32,2,32,4,256]{4,1,0,3,2:T(2,128)(2,1)} %bitcast.129) | data formatting | bytes 8388608 | tf_op jit(solution)/shard_map/reshape | solution.py:65
  136.1 79.5 %all-to-all-done = bf16[2,32,128,256]{3,1,0,2:T(8,128)(2,1)} async-done(((bf16[2,32,128,256]{3,1,0,2:T(8,128)(2,1)}), bf16[2,32,128,256]{3,1,0,2:T(8,128)(2,1)}, u32[]{:S(2)}, u32[]{:S(2)}) %all-to-all-start) | async-done | bytes 4194336 | tf_op jit(solution)/shard_map/all_to_all | solution.py:144
  215.6 8.5 %copy.108 = bf16[2,32,32,4,256]{4,0,2,3,1:T(2,128)(2,1)} copy(bf16[2,32,32,4,256]{4,1,0,3,2:T(8,128)(2,1)} %bitcast.10) | data formatting | bytes 8388608 | tf_op jit(solution)/shard_map/all_to_all | solution.py:144
  224.2 7.3 %reshape.323 = bf16[64,32,2,2,256,1]{4,0,3,2,1,5:T(8,128)(2,1)} reshape(bf16[32,2,32,4,256]{4,1,0,3,2:T(2,128)(2,1)} %bitcast.130) | data formatting | bytes 8388608 | tf_op jit(solution)/shard_map/reshape | solution.py:64
  231.5 3.6 convolution_bitcast_fusion
  235.1 1.3 convolution_bitcast_fusion.1
  236.4 2.4 multiply_convert_fusion.1
  238.8 1.3 fusion.8
  240.1 8.1 %copy.64 = f32[64,32,4,256]{3,1,2,0:T(8,128)} copy(f32[64,32,4,256]{3,0,2,1:T(8,128)S(1)} %bitcast.127) | data formatting | bytes 16777216 | tf_op jit(solution)/shard_map/reshape | solution.py:151
  248.2 6.5 %all-to-all-start.2 = ((f32[64,32,4,256]{3,1,2,0:T(8,128)}), f32[64,32,4,256]{3,1,2,0:T(8,128)}, u32[]{:S(2)}, u32[]{:S(2)}) async-start(f32[64,32,4,256]{3,1,2,0:T(8,128)} %copy.64), calls=%async_computation.2 | async-start | bytes 16777216 | tf_op jit(solution)/shard_map/all_to_all | solution.py:152
  254.8 1.2 reduce-window.14
  256.0 0.2 slice_reduce_fusion.1
  256.2 1.1 reduce-window.16
  257.3 0.2 slice_reduce_fusion
  257.5 0.1 cosine_multiply_fusion
  258.0 12.1 %all-gather = f32[16,8,1]{1,2,0:T(1,128)S(1)} all-gather(f32[2,8,1]{1,2,0:T(1,128)S(1)} %bitcast.139), channel_id=2, replica_groups=mesh['mom'=32,'tm'=8] {'tm'}, dimensions={0}, use_global_device_ids=true | all-gather | bytes 576 | tf_op jit(solution)/shard_map/all_gather | solution.py:19
  270.1 8.5 %all-gather.1 = f32[16,8,1]{1,2,0:T(1,128)S(1)} all-gather(f32[2,8,1]{1,2,0:T(1,128)S(1)} %bitcast.138), channel_id=3, replica_groups=mesh['mom'=32,'tm'=8] {'tm'}, dimensions={0}, use_global_device_ids=true | all-gather | bytes 576 | tf_op jit(solution)/shard_map/all_gather | solution.py:19
  278.7 174.8 %all-to-all-done.2 = f32[64,32,4,256]{3,1,2,0:T(8,128)} async-done(((f32[64,32,4,256]{3,1,2,0:T(8,128)}), f32[64,32,4,256]{3,1,2,0:T(8,128)}, u32[]{:S(2)}, u32[]{:S(2)}) %all-to-all-start.2) | async-done | bytes 8388640 | tf_op jit(solution)/shard_map/all_to_all | solution.py:152
  453.5 4.3 copy.65
  457.8 1.7 fusion.70
  459.5 19.3 %fusion.12 = f32[2,8,256,32,8]{2,3,4,1,0:T(8,128)S(1)} fusion(f32[2,32,8,8,1,256]{5,1,4,3,2,0:T(8,128)S(1)} %get-tuple-element.222, f32[2,8,256]{2,1,0:T(8,128)S(1)} %get-tuple-element.215, f32[2,8,256]{2,1,0:T(8,128)S(1)} %get-tuple-element.214, pred[256,256]{1,0:T(8,128)(4,1)S(1)} %iota_compare_fusion), kind=kOutput, calls=%fused_computation.32 | convolution fusion | flops 3225419776 | bytes 8486912 | tf_op jit(solution)/shard_map/while/body/eval_jaxpr/kRabs,kbsu->kRabu/dot_general | solution.py:84
  478.8 21.4 %fusion.10 = f32[2,8,256,32,8]{2,3,4,1,0:T(8,128)} fusion(f32[2,32,8,8,1,256]{5,1,4,3,2,0:T(8,128)S(1)} %get-tuple-element.223, f32[2,8,256]{2,1,0:T(8,128)S(1)} %get-tuple-element.215, f32[2,8,256]{2,1,0:T(8,128)S(1)} %get-tuple-element.214, pred[256,256]{1,0:T(8,128)(4,1)S(1)} %iota_compare_fusion), kind=kOutput, calls=%fused_computation.31 | convolution fusion | flops 3225419776 | bytes 8486912 | tf_op jit(solution)/shard_map/while/body/eval_jaxpr/kRabs,kbsu->kRabu/dot_general | solution.py:84
  500.2 19.8 %subtract_bitcast_fusion = f32[2,32,8,8,1,256]{5,1,2,3,0,4:T(8,128)S(1)} fusion(f32[2,8,256,32,8]{2,3,4,1,0:T(8,128)S(1)} %fusion.12, f32[2,32,8,8,1,256]{5,1,4,3,2,0:T(8,128)S(1)} %get-tuple-element.223, f32[2,8,256]{2,1,0:T(8,128)S(1)} %get-tuple-element.215, f32[2,8,256]{2,1,0:T(8,128)S(1)} %get-tuple-element.214, pred[256,256]{1,0:T(8,128)(4,1)S(1)} %iota_compare_fusion), kind=kOutput, calls=%fused_computation.25 | convolution fusion | flops 3226468352 | bytes 12681216 | tf_op jit(solution)/shard_map/while/body/eval_jaxpr/kRabs,kbsu->kRabu/dot_general | solution.py:84
  520.0 1.9 copy-done.1
  522.0 0.6 slice.73
  522.6 0.8 copy.72
  523.4 14.8 %all-gather.2 = f32[16,32,8,8,1,1]{1,3,5,4,2,0:T(8,128)S(1)} all-gather(f32[2,32,8,8,1,1]{1,3,5,4,2,0:T(8,128)S(1)} %copy.72), channel_id=4, replica_groups=mesh['mom'=32,'tm'=8] {'tm'}, dimensions={0}, use_global_device_ids=true | all-gather | bytes 147456 | tf_op jit(solution)/shard_map/all_gather | solution.py:19
  538.2 21.8 %add_bitcast_fusion = f32[2,32,8,8,1,256]{5,1,2,3,0,4:T(8,128)S(1)} fusion(f32[2,8,256,32,8]{2,3,4,1,0:T(8,128)} %fusion.10, f32[2,32,8,8,1,256]{5,1,4,3,2,0:T(8,128)} %copy-done.5, f32[2,8,256]{2,1,0:T(8,128)S(1)} %get-tuple-element.215, f32[2,8,256]{2,1,0:T(8,128)S(1)} %get-tuple-element.214, pred[256,256]{1,0:T(8,128)(4,1)S(1)} %iota_compare_fusion), kind=kOutput, calls=%fused_computation.24 | convolution fusion | flops 3226468352 | bytes 12681216 | tf_op jit(solution)/shard_map/while/body/eval_jaxpr/kRabs,kbsu->kRabu/dot_general | solution.py:84
  560.1 2.0 copy-done.3
  562.1 0.6 slice.74
  562.7 0.8 copy.73
  563.5 13.1 %all-gather.3 = f32[16,32,8,8,1,1]{1,3,5,4,2,0:T(8,128)S(1)} all-gather(f32[2,32,8,8,1,1]{1,3,5,4,2,0:T(8,128)S(1)} %copy.73), channel_id=5, replica_groups=mesh['mom'=32,'tm'=8] {'tm'}, dimensions={0}, use_global_device_ids=true | all-gather | bytes 147456 | tf_op jit(solution)/shard_map/all_gather | solution.py:19
  576.6 1.1 while.20
  577.8 1.3 multiply_subtract_fusion
  579.0 0.9 copy-done.2
  579.9 1.3 copy-done.4
  581.2 2.3 fusion.3
  583.6 0.6 copy.76
  584.2 4.5 copy.77
  (44 shorter events, 1.5 us)
Async XLA Ops:
  6.6 106.7 %all-to-all-start.1 = ((bf16[2,32,128,256]{3,1,0,2:T(8,128)(2,1)}), bf16[2,32,128,256]{3,1,0,2:T(8,128)(2,1)}, u32[]{:S(2)}, u32[]{:S(2)}) async-start(bf16[2,32,128,256]{3,1,0,2:T(8,128)(2,1)} %copy.61), calls=%async_computation.1 | async-start | bytes 8388608 | tf_op jit(solution)/shard_map/all_to_all | solution.py:145
  113.3 102.4 %all-to-all-start = ((bf16[2,32,128,256]{3,1,0,2:T(8,128)(2,1)}), bf16[2,32,128,256]{3,1,0,2:T(8,128)(2,1)}, u32[]{:S(2)}, u32[]{:S(2)}) async-start(bf16[2,32,128,256]{3,1,0,2:T(8,128)(2,1)} %copy.59), calls=%async_computation | async-start | bytes 8388608 | tf_op jit(solution)/shard_map/all_to_all | solution.py:144
  231.5 3.6 copy-start
  248.2 6.6 %copy-start.6 = (f32[2,8,256]{2,1,0:T(8,128)S(1)}, f32[2,8,256]{2,1,0:T(8,128)}, u32[]{:S(2)}) copy-start(f32[2,8,256]{2,1,0:T(8,128)} %param.8) | copy-start | bytes 49156
  248.2 7.9 %copy-start.7 = (f32[2,8,256]{2,1,0:T(8,128)S(1)}, f32[2,8,256]{2,1,0:T(8,128)}, u32[]{:S(2)}) copy-start(f32[2,8,256]{2,1,0:T(8,128)} %param.9) | copy-start | bytes 49156
  248.2 205.3 %all-to-all-start.2 = ((f32[64,32,4,256]{3,1,2,0:T(8,128)}), f32[64,32,4,256]{3,1,2,0:T(8,128)}, u32[]{:S(2)}, u32[]{:S(2)}) async-start(f32[64,32,4,256]{3,1,2,0:T(8,128)} %copy.64), calls=%async_computation.2 | async-start | bytes 16777216 | tf_op jit(solution)/shard_map/all_to_all | solution.py:152
  459.4 19.4 %copy-start.5 = (f32[2,32,8,8,1,256]{5,1,4,3,2,0:T(8,128)}, f32[2,32,8,8,1,256]{5,1,4,3,2,0:T(8,128)S(1)}, u32[]{:S(2)}) copy-start(f32[2,32,8,8,1,256]{5,1,4,3,2,0:T(8,128)S(1)} %get-tuple-element.222) | copy-start | bytes 12582916
  520.0 1.9 copy-start.1
  560.0 2.0 copy-start.3
  577.7 2.2 copy-start.2
  577.8 3.5 copy-start.4
where the time goes:
time: 595 us; the launch traced here: 589 us
  waiting for transfers between devices  344 us (58%)
  matrix products  88.6 us (15%)
  local copies, waits for them, and re-layouts  73.5 us (12%)
  blocking collectives  48.5 us (8%)
  starting transfers between devices  23.9 us (4%)
  other arithmetic  9.9 us (2%)
    all_to_all x1, waiting for transfers between devices, shards(): lax.all_to_all(flat, 'mom', split_axis=0, concat_axis=2, tiled=True)  175 us
    all_to_all x1, waiting for transfers between devices, shards(): lax.all_to_all(hole, 'mom', split_axis=2, concat_axis=0, tiled=True)  89.5 us
    dot_general x4, matrix products, apply_kernel(): jnp.einsum('kRabs,kbsu->kRabu', signal, kernel, precision=exact, preferre...  82.4 us
    all_to_all x1, waiting for transfers between devices, shards(): lax.all_to_all(green, 'mom', split_axis=2, concat_axis=0, tiled=True)  79.5 us
    all_gather x4, blocking collectives, prefix(): everything = jax.tree.map(lambda part: lax.all_gather(part, axis), x)  48.5 us
    unnamed x20, local copies, waits for them, and re-layouts  19.4 us
  transfers between devices with their start and end apart: 3, of which 3 were waited for; matrix products, arithmetic and copies ran while one was open for 4% of the time, Pallas kernels for 0%

commit v1 on v0

v1 whole, which is shorter than its diff:
```python
import functools
import math

import jax
import jax.numpy as jnp
import numpy as np
from jax import lax
from jax.experimental import pallas as pl
from jax.experimental.pallas import tpu as pltpu
from jax.sharding import PartitionSpec as P

MESH = pl.DeviceIdType.MESH
F32 = jnp.float32
BF16 = jnp.bfloat16
MOMENTA = 64
ORBITALS = 8
WIDE = 2 * ORBITALS
COUPLING = 0.25
STEP_WEIGHT = 0.0625
LEVELS = 8
ROW_GROUP = 8


def transform_table(handed):
    numbers = np.arange(MOMENTA)
    product = (numbers[:, None] * numbers[None, :]) % MOMENTA
    angles = product.astype(np.float32) * np.float32(2.0 * math.pi / MOMENTA)
    scaled = np.float32(1.0 / math.sqrt(MOMENTA))
    cosine = np.cos(angles) * scaled
    sine = np.float32(handed) * np.sin(angles) * scaled
    return jnp.asarray(np.block([[cosine, -sine], [sine, cosine]]).astype(jnp.bfloat16))


def kernel(
    mom, tm, rows,
    green, hole, decay, phase, plus, minus,
    out,
    gh, sb, rb, tg, th, ts, coef, turn, grow, ends, local, wide, done,
    est, ebox, pst, pbox,
    fwd_send, fwd_recv, ret_send, ret_recv, end_send, end_recv, prod_send, prod_recv, out_sem,
):
    m = lax.axis_index("mom")
    n = lax.axis_index("tm")
    chunks = ORBITALS
    groups = 2 * rows // ROW_GROUP
    per_k = rows // ROW_GROUP

    def field(a):
        return pl.ds(pl.multiple_of(a * WIDE, WIDE), WIDE)

    barrier = pltpu.get_barrier_semaphore()
    ebox[...] = jnp.zeros_like(ebox)
    pbox[...] = jnp.zeros_like(pbox)

    def greet_mom(j, carry):
        pl.semaphore_signal(barrier, inc=1, device_id={"mom": lax.rem(m + j, mom)}, device_id_type=MESH)
        return carry

    def greet_tm(j, carry):
        pl.semaphore_signal(barrier, inc=1, device_id={"tm": lax.rem(n + j, tm)}, device_id_type=MESH)
        return carry

    lax.fori_loop(1, mom, greet_mom, 0)
    lax.fori_loop(1, tm, greet_tm, 0)
    pl.semaphore_wait(barrier, mom + tm - 2)

    def send_fields(a, carry):
        for half, source in enumerate((green, hole)):
            pltpu.make_async_copy(
                source.at[:, m, field(a), :],
                gh.at[a, pl.ds(half * MOMENTA + 2 * m, 2)],
                fwd_recv.at[a],
            ).start()

        def one(j, inner):
            peer = lax.rem(m + j, mom)
            for half, source in enumerate((green, hole)):
                pltpu.make_async_remote_copy(
                    src_ref=source.at[:, peer, field(a), :],
                    dst_ref=gh.at[a, pl.ds(half * MOMENTA + 2 * m, 2)],
                    send_sem=fwd_send.at[a],
                    recv_sem=fwd_recv.at[a],
                    device_id={"mom": peer},
                    device_id_type=MESH,
                ).start()
            return inner

        return lax.fori_loop(1, mom, one, carry)

    lax.fori_loop(0, chunks, send_fields, 0)

    lane = lax.broadcasted_iota(jnp.int32, (ORBITALS, 256), 1)
    sub = lax.broadcasted_iota(jnp.int32, (8, 128), 0)
    col = lax.broadcasted_iota(jnp.int32, (8, 128), 1)
    own_orbital = sub == col % ORBITALS
    real_part = col % WIDE < ORBITALS

    def pattern(column):
        return jnp.sum(jnp.where(own_orbital, column, 0.0), axis=0, keepdims=True)

    def swap_parts(v):
        other = jnp.where(real_part, pltpu.roll(v, 128 - ORBITALS, 1), pltpu.roll(v, ORBITALS, 1))
        return jnp.where(real_part, -other, other)

    last = []
    for k in range(2):
        span = decay[k]
        angle = phase[k]
        for j in range(LEVELS):
            reached = lane >= 2**j
            coef[k, j] = jnp.where(reached, jnp.exp(span), 0.0)
            span = span + jnp.where(reached, pltpu.roll(span, 2**j, 1), 0.0)
            angle = angle + jnp.where(reached, pltpu.roll(angle, 2**j, 1), 0.0)
        cosine, sine, growth = jnp.cos(angle), jnp.sin(angle), jnp.exp(span)
        turn[k, 0] = cosine
        turn[k, 1] = sine
        grow[k] = growth
        last.append([pattern(v[:, 255:256]) for v in (cosine, sine, growth)])
    first_k = sub < per_k
    end_cos, end_sin, end_grow = (jnp.where(first_k, u, v) for u, v in zip(*last))
    ends[0] = end_cos
    ends[1] = end_sin
    pst[0] = end_grow * end_cos
    pst[1] = end_grow * end_sin

    def send_product(j, carry):
        pltpu.make_async_remote_copy(
            src_ref=pst, dst_ref=pbox.at[n], send_sem=prod_send, recv_sem=prod_recv,
            device_id={"tm": lax.rem(n + j, tm)}, device_id_type=MESH,
        ).start()
        return carry

    lax.fori_loop(1, tm, send_product, 0)

    def work(a, carry):
        pltpu.make_async_copy(gh.at[a], gh.at[a], fwd_recv.at[a]).wait()
        for h in range(2):
            lanes = slice(128 * h, 128 * h + 128)
            tg[h] = gh[a, 0:MOMENTA, :, lanes].astype(F32).reshape(MOMENTA * WIDE, 128)
            th[h] = gh[a, MOMENTA:, :, lanes].astype(F32).reshape(MOMENTA * WIDE, 128)

        def gather(ref, row):
            parts = [
                jnp.concatenate([ref[h, pl.ds(row + c, MOMENTA, stride=WIDE), :] for h in range(2)], axis=1)
                for c in range(2)
            ]
            return jnp.concatenate(parts, axis=0).astype(BF16)

        for b in range(ORBITALS):
            g = jnp.dot(plus[...], gather(tg, 2 * b), preferred_element_type=F32)
            q = jnp.dot(minus[...], gather(th, 2 * b), preferred_element_type=F32)
            g_re, g_im = g[:MOMENTA], g[MOMENTA:]
            q_re, q_im = q[:MOMENTA], q[MOMENTA:]
            square_re = g_re * g_re - g_im * g_im
            square_im = 2.0 * g_re * g_im
            energy_re = COUPLING * (square_re * q_re - square_im * q_im)
            energy_im = COUPLING * (square_re * q_im + square_im * q_re)
            energy = jnp.concatenate([energy_re, energy_im], axis=0).astype(BF16)
            back = jnp.dot(minus[...], energy, preferred_element_type=F32)
            for h in range(2):
                lanes = slice(128 * h, 128 * h + 128)
                for c in range(2):
                    ts[h, pl.ds(c * ORBITALS + b, MOMENTA, stride=WIDE), :] = back[
                        c * MOMENTA : (c + 1) * MOMENTA, lanes
                    ]
        for h in range(2):
            sb[a, :, :, 128 * h : 128 * h + 128] = ts[h].reshape(MOMENTA, WIDE, 128).astype(BF16)

        pltpu.make_async_copy(sb.at[a, pl.ds(2 * m, 2)], rb.at[a, m], ret_recv.at[a]).start()

        def one(j, inner):
            peer = lax.rem(m + j, mom)
            pltpu.make_async_remote_copy(
                src_ref=sb.at[a, pl.ds(2 * peer, 2)],
                dst_ref=rb.at[a, m],
                send_sem=ret_send.at[a],
                recv_sem=ret_recv.at[a],
                device_id={"mom": peer},
                device_id_type=MESH,
            ).start()
            return inner

        return lax.fori_loop(1, mom, one, carry)

    lax.fori_loop(0, chunks, work, 0)

    def scan_chunk(a):
        slot = a % 2
        pltpu.make_async_copy(rb.at[a], rb.at[a], ret_recv.at[a]).wait()

        def group(i, total):
            k = i // per_k
            t = pl.multiple_of((i % per_k) * ROW_GROUP, ROW_GROUP)
            x = rb[a, pl.ds(t, ROW_GROUP), k].astype(F32)
            x_re, x_im = x[:, :ORBITALS], x[:, ORBITALS:]
            cosine, sine = turn[k, 0], turn[k, 1]
            y_re = cosine * x_re + sine * x_im
            y_im = cosine * x_im - sine * x_re
            for j in range(LEVELS):
                factor = coef[k, j]
                y_re = y_re + factor * pltpu.roll(y_re, 2**j, 2)
                y_im = y_im + factor * pltpu.roll(y_im, 2**j, 2)
            y = jnp.concatenate([y_re, y_im], axis=1)
            local[slot, k, pl.ds(t, ROW_GROUP)] = y
            tail = y.reshape(ROW_GROUP * WIDE, 256)[:, 128:]
            row = jnp.transpose(tail)[127:128, :]
            return jnp.where(sub == i, row, total)

        total = lax.fori_loop(0, groups, group, jnp.zeros((8, 128), F32))
        est[a] = ends[0] * total + ends[1] * swap_parts(total)

        def one(j, carry):
            pltpu.make_async_remote_copy(
                src_ref=est.at[a], dst_ref=ebox.at[a, n], send_sem=end_send.at[a], recv_sem=end_recv.at[a],
                device_id={"tm": lax.rem(n + j, tm)}, device_id_type=MESH,
            ).start()
            return carry

        lax.fori_loop(1, tm, one, 0)

    def finish_chunk(a):
        slot = a % 2
        pltpu.make_async_copy(ebox.at[a, pl.ds(0, tm - 1)], ebox.at[a, pl.ds(0, tm - 1)], end_recv.at[a]).wait()
        enter = jnp.zeros((8, 128), F32)
        for j in range(tm - 1):
            moved = pbox[j, 0] * enter + pbox[j, 1] * swap_parts(enter) + ebox[a, j]
            enter = jnp.where(j < n, moved, enter)
        columns = jnp.transpose(jnp.concatenate([enter, jnp.zeros((120, 128), F32)], axis=0))

        @pl.when(a >= 2)
        def _():
            pltpu.make_async_copy(done.at[slot], out.at[:, :, field(a), :], out_sem.at[slot]).wait()

        for i in range(groups):
            k, t = i // per_k, (i % per_k) * ROW_GROUP
            column = columns[:, i : i + 1].reshape(ROW_GROUP, WIDE, 1)
            r = local[slot, k, t : t + ROW_GROUP]
            growth = grow[k]
            cosine, sine = STEP_WEIGHT * turn[k, 0], STEP_WEIGHT * turn[k, 1]
            r_re = r[:, :ORBITALS] + column[:, :ORBITALS] * growth
            r_im = r[:, ORBITALS:] + column[:, ORBITALS:] * growth
            h_re = (cosine * r_re - sine * r_im).reshape(ROW_GROUP * ORBITALS, 256)
            h_im = (cosine * r_im + sine * r_re).reshape(ROW_GROUP * ORBITALS, 256)
            for h in range(2):
                lanes = slice(128 * h, 128 * h + 128)
                wide[i, h, pl.ds(0, ROW_GROUP * ORBITALS, stride=2), :] = h_re[:, lanes]
                wide[i, h, pl.ds(1, ROW_GROUP * ORBITALS, stride=2), :] = h_im[:, lanes]
                done[slot, k, t : t + ROW_GROUP, :, lanes] = (
                    wide[i, h].reshape(ROW_GROUP, WIDE, 128).astype(BF16)
                )
        pltpu.make_async_copy(done.at[slot], out.at[:, :, field(a), :], out_sem.at[slot]).start()

    pltpu.make_async_copy(pbox.at[pl.ds(0, tm - 1)], pbox.at[pl.ds(0, tm - 1)], prod_recv).wait()

    def history(a, carry):
        scan_chunk(a)

        @pl.when(a >= 1)
        def _():
            finish_chunk(a - 1)

        return carry

    lax.fori_loop(0, chunks, history, 0)
    finish_chunk(jnp.int32(chunks - 1))

    def drain(a, carry):
        pltpu.make_async_copy(gh.at[a, pl.ds(0, 4 * mom - 4)], gh.at[a, pl.ds(0, 4 * mom - 4)], fwd_send.at[a]).wait()
        pltpu.make_async_copy(rb.at[a, pl.ds(0, mom - 1)], rb.at[a, pl.ds(0, mom - 1)], ret_send.at[a]).wait()
        pltpu.make_async_copy(ebox.at[a, pl.ds(0, tm - 1)], ebox.at[a, pl.ds(0, tm - 1)], end_send.at[a]).wait()
        return carry

    lax.fori_loop(0, chunks, drain, 0)
    pltpu.make_async_copy(pbox.at[pl.ds(0, tm - 1)], pbox.at[pl.ds(0, tm - 1)], prod_send).wait()
    for slot in range(2):
        pltpu.make_async_copy(done.at[slot], out.at[:, :, field(0), :], out_sem.at[slot]).wait()


def solution(mesh):
    mom, tm = mesh.shape["mom"], mesh.shape["tm"]

    def shards(green, hole, decay_log, phase_step):
        rows = green.shape[1]
        chunks = ORBITALS
        vmem = pl.BlockSpec(memory_space=pltpu.VMEM)
        anywhere = pl.BlockSpec(memory_space=pl.ANY)
        dma = pltpu.SemaphoreType.DMA
        return pl.pallas_call(
            functools.partial(kernel, mom, tm, rows),
            out_shape=jax.ShapeDtypeStruct(green.shape, BF16),
            in_specs=[anywhere, anywhere, vmem, vmem, vmem, vmem],
            out_specs=anywhere,
            scratch_shapes=[
                pltpu.VMEM((chunks, 2 * MOMENTA, WIDE, 256), BF16),
                pltpu.VMEM((chunks, MOMENTA, WIDE, 256), BF16),
                pltpu.VMEM((chunks, mom, 2, WIDE, 256), BF16),
                pltpu.VMEM((2, MOMENTA * WIDE, 128), F32),
                pltpu.VMEM((2, MOMENTA * WIDE, 128), F32),
                pltpu.VMEM((2, MOMENTA * WIDE, 128), F32),
                pltpu.VMEM((2, LEVELS, ORBITALS, 256), F32),
                pltpu.VMEM((2, 2, ORBITALS, 256), F32),
                pltpu.VMEM((2, ORBITALS, 256), F32),
                pltpu.VMEM((2, 8, 128), F32),
                pltpu.VMEM((2, 2, rows, WIDE, 256), F32),
                pltpu.VMEM((2 * rows // ROW_GROUP, 2, ROW_GROUP * WIDE, 128), F32),
                pltpu.VMEM((2, 2, rows, WIDE, 256), BF16),
                pltpu.VMEM((chunks, 8, 128), F32),
                pltpu.VMEM((chunks, tm, 8, 128), F32),
                pltpu.VMEM((2, 8, 128), F32),
                pltpu.VMEM((tm, 2, 8, 128), F32),
                dma((chunks,)), dma((chunks,)), dma((chunks,)), dma((chunks,)),
                dma((chunks,)), dma((chunks,)), dma(()), dma(()), dma((2,)),
            ],
            compiler_params=pltpu.CompilerParams(
                collective_id=0, has_side_effects=True, vmem_limit_bytes=56 << 20
            ),
        )(green, hole, decay_log, phase_step, transform_table(1.0), transform_table(-1.0))

    in_specs = (
        P("mom", None, None, "tm"),
        P("mom", None, None, "tm"),
        P("mom", None, "tm"),
        P("mom", None, "tm"),
    )
    out_specs = P("mom", None, None, "tm")
    return jax.shard_map(shards, mesh=mesh, in_specs=in_specs, out_specs=out_specs, check_vma=False)
```

time: 595 us -> 301 us (0.51)
  waiting for transfers between devices: 344 us -> 0 us
  Pallas kernels: 0 us -> 294 us
  matrix products: 88.6 us -> 0 us
  local copies, waits for them, and re-layouts: 73.5 us -> 4.7 us
  blocking collectives: 48.5 us -> 0 us
  starting transfers between devices: 23.9 us -> 0 us
  other arithmetic: 9.9 us -> 0 us
    all_to_all x3 -> x0, waiting for transfers between devices: 344 us -> none  [the longest x1 175 us: shards(): lax.all_to_all(flat, 'mom', split_axis=0, concat_axis=2, tiled=True)]
    pallas_call x0 -> x1, Pallas kernels: none -> 294 us  [shards(): pl.pallas_call(functools.partial(kernel, mom, tm, rows), out_shape=jax.Sh...]
    dot_general x7 -> x0, matrix products: 88.6 us -> none  [the longest x4 82.4 us: apply_kernel(): jnp.einsum('kRabs,kbsu->kRabu', signal, kernel, precision=exact, preferre...]
    all_gather x4 -> x0, blocking collectives: 48.5 us -> none  [prefix(): everything = jax.tree.map(lambda part: lax.all_gather(part, axis), x)]
    all_to_all x3 -> x0, starting transfers between devices: 23.9 us -> none  [the longest x1 10.7 us: shards(): lax.all_to_all(hole, 'mom', split_axis=2, concat_axis=0, tiled=True)]
    reshape x3 -> x0, local copies, waits for them, and re-layouts: 22.6 us -> none  [the longest x1 8.08 us: shards(): flat = energy.reshape(momenta, row_count, pair_width * two_parts, columns)]
    all_to_all x3 -> x0, local copies, waits for them, and re-layouts: 21.3 us -> none  [the longest x1 8.52 us: shards(): lax.all_to_all(hole, 'mom', split_axis=2, concat_axis=0, tiled=True)]
    unnamed x20 -> x1, local copies, waits for them, and re-layouts: 19.4 us -> 4.7 us
  transfers between devices with their start and end apart: 3 -> 0, of which waited for: 3 -> 0; matrix products, arithmetic and copies ran while one was open for 4% -> 0% of each run, Pallas kernels for 0% -> 0%
where the time goes in v1:
time: 301 us; the launch traced here: 298 us
  Pallas kernels  294 us (98%)
  local copies, waits for them, and re-layouts  4.7 us (2%)
    pallas_call x1, Pallas kernels, shards(): pl.pallas_call(functools.partial(kernel, mom, tm, rows), out_shape=jax.Sh...  294 us

profile of v1, /device:TPU:33, one launch (start us, length us, event | category | flops | bytes accessed | tf_op | source)
XLA Modules:
  0.0 298.4 jit_solution(6881508989956322596)
XLA Ops:
  0.0 293.7 %shard_map.64 = bf16[2,32,128,256]{3,2,1,0:T(8,128)(2,1)} custom-call(bf16[2,32,128,256]{3,2,1,0:T(8,128)(2,1)} %green.1, bf16[2,32,128,256]{3,2,1,0:T(8,128)(2,1)} %hole.1, f32[2,8,256]{2,1,0:T(8,128)} %decay.1, f32[2,8,256]{2,1,0:T(8,128)} %phase.1, bf16[128,128]{1,0:T(8,128)(2,1)} %constant.4.clone.plus, bf16[128,128]{1,0:T(8,128)(2,1)} %constant.5.clone.minus), custom_call_target="tpu_custom_call" | custom-call | tf_op jit(solution)/shard_map/pallas_call | solution.py:288
  293.7 4.7 %copy.8 = bf16[2,32,128,256]{3,2,1,0:T(8,128)(2,1)} copy(bf16[2,32,128,256]{3,2,1,0:T(8,128)(2,1)} %shard_map.64) | data formatting | bytes 8388608

commit v2 on v1

--- a/solution.py
+++ b/solution.py
@@ -35,15 +35,32 @@
     mom, tm, rows,
     green, hole, decay, phase, plus, minus,
     out,
-    gh, sb, rb, tg, th, ts, coef, turn, grow, ends, local, wide, done,
+    gh, sb, rb, tg, th, ts, coef, turn, grow, ends, local, wide,
     est, ebox, pst, pbox,
-    fwd_send, fwd_recv, ret_send, ret_recv, end_send, end_recv, prod_send, prod_recv, out_sem,
+    fwd_send, fwd_recv, ret_send, ret_recv, end_send, end_recv, prod_send, prod_recv,
 ):
     m = lax.axis_index("mom")
     n = lax.axis_index("tm")
     chunks = ORBITALS
     groups = 2 * rows // ROW_GROUP
     per_k = rows // ROW_GROUP
+    side = 8
+    across = mom // side
+    x, z = m // side, m % side
+
+    def offset(j):
+        q, i = j // 8, j % 8
+        turned = i // 4
+        dz = jnp.where(q == 0, 4 * turned, (4 - q) * (1 - 2 * turned))
+        return i % 4, dz
+
+    def target(j):
+        dx, dz = offset(j)
+        return lax.rem(x + dx, across) * side + lax.rem(z + dz + side, side)
+
+    def origin(j):
+        dx, dz = offset(j)
+        return lax.rem(x - dx + across, across) * side + lax.rem(z - dz + side, side)
 
     def field(a):
         return pl.ds(pl.multiple_of(a * WIDE, WIDE), WIDE)
@@ -73,7 +90,7 @@
             ).start()
 
         def one(j, inner):
-            peer = lax.rem(m + j, mom)
+            peer = target(j)
             for half, source in enumerate((green, hole)):
                 pltpu.make_async_remote_copy(
                     src_ref=source.at[:, peer, field(a), :],
@@ -92,6 +109,7 @@
     lane = lax.broadcasted_iota(jnp.int32, (ORBITALS, 256), 1)
     sub = lax.broadcasted_iota(jnp.int32, (8, 128), 0)
     col = lax.broadcasted_iota(jnp.int32, (8, 128), 1)
+    near = lax.broadcasted_iota(jnp.int32, (ROW_GROUP, ORBITALS, 128), 2)
     own_orbital = sub == col % ORBITALS
     real_part = col % WIDE < ORBITALS
 
@@ -166,15 +184,15 @@
         for h in range(2):
             sb[a, :, :, 128 * h : 128 * h + 128] = ts[h].reshape(MOMENTA, WIDE, 128).astype(BF16)
 
-        pltpu.make_async_copy(sb.at[a, pl.ds(2 * m, 2)], rb.at[a, m], ret_recv.at[a]).start()
+        pltpu.make_async_copy(sb.at[a, pl.ds(2 * m, 2)], rb.at[a, 0], ret_recv.at[a, 0]).start()
 
         def one(j, inner):
-            peer = lax.rem(m + j, mom)
+            peer = target(j)
             pltpu.make_async_remote_copy(
                 src_ref=sb.at[a, pl.ds(2 * peer, 2)],
-                dst_ref=rb.at[a, m],
+                dst_ref=rb.at[a, j],
                 send_sem=ret_send.at[a],
-                recv_sem=ret_recv.at[a],
+                recv_sem=ret_recv.at[a, j // ROW_GROUP],
                 device_id={"mom": peer},
                 device_id_type=MESH,
             ).start()
@@ -186,27 +204,36 @@
 
     def scan_chunk(a):
         slot = a % 2
-        pltpu.make_async_copy(rb.at[a], rb.at[a], ret_recv.at[a]).wait()
-
-        def group(i, total):
-            k = i // per_k
-            t = pl.multiple_of((i % per_k) * ROW_GROUP, ROW_GROUP)
-            x = rb[a, pl.ds(t, ROW_GROUP), k].astype(F32)
-            x_re, x_im = x[:, :ORBITALS], x[:, ORBITALS:]
-            cosine, sine = turn[k, 0], turn[k, 1]
-            y_re = cosine * x_re + sine * x_im
-            y_im = cosine * x_im - sine * x_re
-            for j in range(LEVELS):
-                factor = coef[k, j]
-                y_re = y_re + factor * pltpu.roll(y_re, 2**j, 2)
-                y_im = y_im + factor * pltpu.roll(y_im, 2**j, 2)
-            y = jnp.concatenate([y_re, y_im], axis=1)
-            local[slot, k, pl.ds(t, ROW_GROUP)] = y
-            tail = y.reshape(ROW_GROUP * WIDE, 256)[:, 128:]
-            row = jnp.transpose(tail)[127:128, :]
-            return jnp.where(sub == i, row, total)
-
-        total = lax.fori_loop(0, groups, group, jnp.zeros((8, 128), F32))
+
+        def group(q, total):
+            t = pl.multiple_of(q * ROW_GROUP, ROW_GROUP)
+            block = rb.at[a, pl.ds(t, ROW_GROUP)]
+            pltpu.make_async_copy(block, block, ret_recv.at[a, q]).wait()
+            for k in range(2):
+                v = rb[a, pl.ds(t, ROW_GROUP), k].astype(F32)
+                cosine, sine = turn[k, 0], turn[k, 1]
+                v_re, v_im = v[:, :ORBITALS], v[:, ORBITALS:]
+                y_re = cosine * v_re + sine * v_im
+                y_im = cosine * v_im - sine * v_re
+                parts = []
+                for y in (y_re, y_im):
+                    lo, hi = y[:, :, :128], y[:, :, 128:]
+                    for j in range(LEVELS - 1):
+                        factor = coef[k, j]
+                        lo_moved, hi_moved = pltpu.roll(lo, 2**j, 2), pltpu.roll(hi, 2**j, 2)
+                        hi = hi + factor[:, 128:] * jnp.where(near >= 2**j, hi_moved, lo_moved)
+                        lo = lo + factor[:, :128] * lo_moved
+                    hi = hi + coef[k, LEVELS - 1][:, 128:] * lo
+                    parts.append((lo, hi))
+                los = jnp.concatenate([parts[0][0], parts[1][0]], axis=1)
+                his = jnp.concatenate([parts[0][1], parts[1][1]], axis=1)
+                local[slot, k, pl.ds(t, ROW_GROUP), :, 0:128] = los
+                local[slot, k, pl.ds(t, ROW_GROUP), :, 128:256] = his
+                row = jnp.transpose(his.reshape(ROW_GROUP * WIDE, 128))[127:128, :]
+                total = jnp.where(sub == k * per_k + q, row, total)
+            return total
+
+        total = lax.fori_loop(0, per_k, group, jnp.zeros((8, 128), F32))
         est[a] = ends[0] * total + ends[1] * swap_parts(total)
 
         def one(j, carry):
@@ -226,10 +253,6 @@
             moved = pbox[j, 0] * enter + pbox[j, 1] * swap_parts(enter) + ebox[a, j]
             enter = jnp.where(j < n, moved, enter)
         columns = jnp.transpose(jnp.concatenate([enter, jnp.zeros((120, 128), F32)], axis=0))
-
-        @pl.when(a >= 2)
-        def _():
-            pltpu.make_async_copy(done.at[slot], out.at[:, :, field(a), :], out_sem.at[slot]).wait()
 
         for i in range(groups):
             k, t = i // per_k, (i % per_k) * ROW_GROUP
@@ -245,10 +268,9 @@
                 lanes = slice(128 * h, 128 * h + 128)
                 wide[i, h, pl.ds(0, ROW_GROUP * ORBITALS, stride=2), :] = h_re[:, lanes]
                 wide[i, h, pl.ds(1, ROW_GROUP * ORBITALS, stride=2), :] = h_im[:, lanes]
-                done[slot, k, t : t + ROW_GROUP, :, lanes] = (
-                    wide[i, h].reshape(ROW_GROUP, WIDE, 128).astype(BF16)
-                )
-        pltpu.make_async_copy(done.at[slot], out.at[:, :, field(a), :], out_sem.at[slot]).start()
+                whole = wide[i, h].reshape(ROW_GROUP, WIDE, 128).astype(BF16)
+                for e in range(ROW_GROUP):
+                    out[k, origin(t + e), field(a), lanes] = whole[e]
 
     pltpu.make_async_copy(pbox.at[pl.ds(0, tm - 1)], pbox.at[pl.ds(0, tm - 1)], prod_recv).wait()
 
@@ -272,8 +294,6 @@
 
     lax.fori_loop(0, chunks, drain, 0)
     pltpu.make_async_copy(pbox.at[pl.ds(0, tm - 1)], pbox.at[pl.ds(0, tm - 1)], prod_send).wait()
-    for slot in range(2):
-        pltpu.make_async_copy(done.at[slot], out.at[:, :, field(0), :], out_sem.at[slot]).wait()
 
 
 def solution(mesh):
@@ -287,9 +307,9 @@
         dma = pltpu.SemaphoreType.DMA
         return pl.pallas_call(
             functools.partial(kernel, mom, tm, rows),
-            out_shape=jax.ShapeDtypeStruct(green.shape, BF16),
+            out_shape=pltpu.VMEM(green.shape, BF16),
             in_specs=[anywhere, anywhere, vmem, vmem, vmem, vmem],
-            out_specs=anywhere,
+            out_specs=vmem,
             scratch_shapes=[
                 pltpu.VMEM((chunks, 2 * MOMENTA, WIDE, 256), BF16),
                 pltpu.VMEM((chunks, MOMENTA, WIDE, 256), BF16),
@@ -303,13 +323,12 @@
                 pltpu.VMEM((2, 8, 128), F32),
                 pltpu.VMEM((2, 2, rows, WIDE, 256), F32),
                 pltpu.VMEM((2 * rows // ROW_GROUP, 2, ROW_GROUP * WIDE, 128), F32),
-                pltpu.VMEM((2, 2, rows, WIDE, 256), BF16),
                 pltpu.VMEM((chunks, 8, 128), F32),
                 pltpu.VMEM((chunks, tm, 8, 128), F32),
                 pltpu.VMEM((2, 8, 128), F32),
                 pltpu.VMEM((tm, 2, 8, 128), F32),
-                dma((chunks,)), dma((chunks,)), dma((chunks,)), dma((chunks,)),
-                dma((chunks,)), dma((chunks,)), dma(()), dma(()), dma((2,)),
+                dma((chunks,)), dma((chunks,)), dma((chunks,)), dma((chunks, rows // ROW_GROUP)),
+                dma((chunks,)), dma((chunks,)), dma(()), dma(()),
             ],
             compiler_params=pltpu.CompilerParams(
                 collective_id=0, has_side_effects=True, vmem_limit_bytes=56 << 20

time: 301 us -> 293 us (0.973)
  Pallas kernels: 294 us -> 290 us
    pallas_call x1, Pallas kernels: 294 us -> 290 us  [shards(): pl.pallas_call(functools.partial(kernel, mom, tm, rows), out_shape=pltpu....]
where the time goes in v2:
time: 293 us; the launch traced here: 292 us
  Pallas kernels  290 us (99%)
    pallas_call x1, Pallas kernels, shards(): pl.pallas_call(functools.partial(kernel, mom, tm, rows), out_shape=pltpu....  290 us

profile of v2, /device:TPU:33, one launch (start us, length us, event | category | flops | bytes accessed | tf_op | source)
XLA Modules:
  0.0 291.8 jit_solution(11583226635524926694)
XLA Ops:
  0.0 289.8 %shard_map.64 = bf16[2,32,128,256]{3,2,1,0:T(8,128)(2,1)S(1)} custom-call(bf16[2,32,128,256]{3,2,1,0:T(8,128)(2,1)} %green.1, bf16[2,32,128,256]{3,2,1,0:T(8,128)(2,1)} %hole.1, f32[2,8,256]{2,1,0:T(8,128)} %decay.1, f32[2,8,256]{2,1,0:T(8,128)} %phase.1, bf16[128,128]{1,0:T(8,128)(2,1)} %constant.4.clone.plus, bf16[128,128]{1,0:T(8,128)(2,1)} %constant.5.clone.minus), custom_call_target="tpu_custom_call" | custom-call | tf_op jit(solution)/shard_map/pallas_call | solution.py:308
  289.8 2.0 copy.8

commit v3 on v2

--- a/solution.py
+++ b/solution.py
@@ -35,9 +35,9 @@
     mom, tm, rows,
     green, hole, decay, phase, plus, minus,
     out,
-    gh, sb, rb, tg, th, ts, coef, turn, grow, ends, local, wide,
+    gh, sb, rb, tg, th, ts, coef, turn, grow, heavy, reach, local, wide,
     est, ebox, pst, pbox,
-    fwd_send, fwd_recv, ret_send, ret_recv, end_send, end_recv, prod_send, prod_recv,
+    fwd_send, fwd_recv, ret_send, ret_recv, end_send, end_recv, prod_send, prod_recv, line_z, line_x,
 ):
     m = lax.axis_index("mom")
     n = lax.axis_index("tm")
@@ -69,19 +69,44 @@
     ebox[...] = jnp.zeros_like(ebox)
     pbox[...] = jnp.zeros_like(pbox)
 
-    def greet_mom(j, carry):
-        pl.semaphore_signal(barrier, inc=1, device_id={"mom": lax.rem(m + j, mom)}, device_id_type=MESH)
-        return carry
+    def at(dx, dz):
+        return lax.rem(x + dx + across, across) * side + lax.rem(z + dz + side, side)
+
+    def greet(semaphore, **where):
+        pl.semaphore_signal(semaphore, inc=1, device_id=where, device_id_type=MESH)
+
+    for dz in (1, -1, 2, -2):
+        greet(barrier, mom=at(0, dz))
+    for dx in range(1, across):
+        greet(barrier, mom=at(dx, 0))
 
     def greet_tm(j, carry):
-        pl.semaphore_signal(barrier, inc=1, device_id={"tm": lax.rem(n + j, tm)}, device_id_type=MESH)
-        return carry
-
-    lax.fori_loop(1, mom, greet_mom, 0)
+        greet(barrier, tm=lax.rem(n + j, tm))
+        return carry
+
     lax.fori_loop(1, tm, greet_tm, 0)
-    pl.semaphore_wait(barrier, mom + tm - 2)
-
-    def send_fields(a, carry):
+    pl.semaphore_wait(barrier, 4 + across - 1 + tm - 1)
+    for dz in (2, -2):
+        greet(line_z, mom=at(0, dz))
+
+    def send_field(a, j):
+        peer = target(j)
+        for half, source in enumerate((green, hole)):
+            pltpu.make_async_remote_copy(
+                src_ref=source.at[:, peer, field(a), :],
+                dst_ref=gh.at[a, pl.ds(half * MOMENTA + 2 * m, 2)],
+                send_sem=fwd_send.at[a],
+                recv_sem=fwd_recv.at[a],
+                device_id={"mom": peer},
+                device_id_type=MESH,
+            ).start()
+
+    def send_near(a, carry):
+        for j in (16, 20, 24, 28):
+            send_field(a, j)
+        return carry
+
+    def send_far(a, carry):
         for half, source in enumerate((green, hole)):
             pltpu.make_async_copy(
                 source.at[:, m, field(a), :],
@@ -90,21 +115,20 @@
             ).start()
 
         def one(j, inner):
-            peer = target(j)
-            for half, source in enumerate((green, hole)):
-                pltpu.make_async_remote_copy(
-                    src_ref=source.at[:, peer, field(a), :],
-                    dst_ref=gh.at[a, pl.ds(half * MOMENTA + 2 * m, 2)],
-                    send_sem=fwd_send.at[a],
-                    recv_sem=fwd_recv.at[a],
-                    device_id={"mom": peer},
-                    device_id_type=MESH,
-                ).start()
+            @pl.when(jnp.logical_or(j < 16, j % 4 != 0))
+            def _():
+                send_field(a, j)
+
             return inner
 
         return lax.fori_loop(1, mom, one, carry)
 
-    lax.fori_loop(0, chunks, send_fields, 0)
+    lax.fori_loop(0, chunks, send_near, 0)
+    pl.semaphore_wait(line_z, 2)
+    for dx in range(1, across):
+        greet(line_x, mom=at(dx, 0))
+    pl.semaphore_wait(line_x, across - 1)
+    lax.fori_loop(0, chunks, send_far, 0)
 
     lane = lax.broadcasted_iota(jnp.int32, (ORBITALS, 256), 1)
     sub = lax.broadcasted_iota(jnp.int32, (8, 128), 0)
@@ -130,14 +154,20 @@
             span = span + jnp.where(reached, pltpu.roll(span, 2**j, 1), 0.0)
             angle = angle + jnp.where(reached, pltpu.roll(angle, 2**j, 1), 0.0)
         cosine, sine, growth = jnp.cos(angle), jnp.sin(angle), jnp.exp(span)
+        rest = jnp.where(lane < 255, pltpu.roll(decay[k], 255, 1), 0.0)
+        for j in range(LEVELS):
+            rest = rest + jnp.where(lane < 256 - 2**j, pltpu.roll(rest, 256 - 2**j, 1), 0.0)
+        fade = jnp.exp(rest)
+        to_turn = angle[:, 255:256] - angle
+        weight = jnp.concatenate([fade * jnp.cos(to_turn), fade * jnp.sin(to_turn)], axis=0)
+        high = weight.astype(BF16)
+        heavy[k] = jnp.concatenate([high, (weight - high.astype(F32)).astype(BF16)], axis=0)
         turn[k, 0] = cosine
         turn[k, 1] = sine
         grow[k] = growth
         last.append([pattern(v[:, 255:256]) for v in (cosine, sine, growth)])
     first_k = sub < per_k
     end_cos, end_sin, end_grow = (jnp.where(first_k, u, v) for u, v in zip(*last))
-    ends[0] = end_cos
-    ends[1] = end_sin
     pst[0] = end_grow * end_cos
     pst[1] = end_grow * end_sin
 
@@ -205,10 +235,33 @@
     def scan_chunk(a):
         slot = a % 2
 
-        def group(q, total):
+        def ending(q, total):
             t = pl.multiple_of(q * ROW_GROUP, ROW_GROUP)
             block = rb.at[a, pl.ds(t, ROW_GROUP)]
             pltpu.make_async_copy(block, block, ret_recv.at[a, q]).wait()
+            for k in range(2):
+                v = rb[a, pl.ds(t, ROW_GROUP), k].reshape(ROW_GROUP * WIDE, 256)
+                r = lax.dot_general(heavy[k], v, (((1,), (1,)), ((), ())), preferred_element_type=F32)
+                r = r[:WIDE] + r[WIDE:]
+                p = jnp.sum(jnp.where(own_orbital, r[:ORBITALS], 0.0), axis=0, keepdims=True)
+                w = jnp.sum(jnp.where(own_orbital, r[ORBITALS:], 0.0), axis=0, keepdims=True)
+                row = p + swap_parts(jnp.broadcast_to(w, (8, 128)))
+                total = jnp.where(sub == k * per_k + q, row, total)
+            return total
+
+        est[a] = lax.fori_loop(0, per_k, ending, jnp.zeros((8, 128), F32))
+
+        def one(j, carry):
+            pltpu.make_async_remote_copy(
+                src_ref=est.at[a], dst_ref=ebox.at[a, n], send_sem=end_send.at[a], recv_sem=end_recv.at[a],
+                device_id={"tm": lax.rem(n + j, tm)}, device_id_type=MESH,
+            ).start()
+            return carry
+
+        lax.fori_loop(1, tm, one, 0)
+
+        def group(q, carry):
+            t = pl.multiple_of(q * ROW_GROUP, ROW_GROUP)
             for k in range(2):
                 v = rb[a, pl.ds(t, ROW_GROUP), k].astype(F32)
                 cosine, sine = turn[k, 0], turn[k, 1]
@@ -229,29 +282,16 @@
                 his = jnp.concatenate([parts[0][1], parts[1][1]], axis=1)
                 local[slot, k, pl.ds(t, ROW_GROUP), :, 0:128] = los
                 local[slot, k, pl.ds(t, ROW_GROUP), :, 128:256] = his
-                row = jnp.transpose(his.reshape(ROW_GROUP * WIDE, 128))[127:128, :]
-                total = jnp.where(sub == k * per_k + q, row, total)
-            return total
-
-        total = lax.fori_loop(0, per_k, group, jnp.zeros((8, 128), F32))
-        est[a] = ends[0] * total + ends[1] * swap_parts(total)
-
-        def one(j, carry):
-            pltpu.make_async_remote_copy(
-                src_ref=est.at[a], dst_ref=ebox.at[a, n], send_sem=end_send.at[a], recv_sem=end_recv.at[a],
-                device_id={"tm": lax.rem(n + j, tm)}, device_id_type=MESH,
-            ).start()
             return carry
 
-        lax.fori_loop(1, tm, one, 0)
+        lax.fori_loop(0, per_k, group, 0)
 
     def finish_chunk(a):
         slot = a % 2
         pltpu.make_async_copy(ebox.at[a, pl.ds(0, tm - 1)], ebox.at[a, pl.ds(0, tm - 1)], end_recv.at[a]).wait()
         enter = jnp.zeros((8, 128), F32)
         for j in range(tm - 1):
-            moved = pbox[j, 0] * enter + pbox[j, 1] * swap_parts(enter) + ebox[a, j]
-            enter = jnp.where(j < n, moved, enter)
+            enter = enter + (reach[j, 0] * ebox[a, j] + reach[j, 1] * swap_parts(ebox[a, j]))
         columns = jnp.transpose(jnp.concatenate([enter, jnp.zeros((120, 128), F32)], axis=0))
 
         for i in range(groups):
@@ -273,6 +313,16 @@
                     out[k, origin(t + e), field(a), lanes] = whole[e]
 
     pltpu.make_async_copy(pbox.at[pl.ds(0, tm - 1)], pbox.at[pl.ds(0, tm - 1)], prod_recv).wait()
+    through_re, through_im = jnp.ones((8, 128), F32), jnp.zeros((8, 128), F32)
+    for j in range(tm - 2, -1, -1):
+        p_re, p_im = pbox[j, 0], pbox[j, 1]
+        earlier = j < n
+        reach[j, 0] = jnp.where(earlier, through_re, 0.0)
+        reach[j, 1] = jnp.where(earlier, through_im, 0.0)
+        through_re, through_im = (
+            jnp.where(earlier, through_re * p_re - through_im * p_im, through_re),
+            jnp.where(earlier, through_re * p_im + through_im * p_re, through_im),
+        )
 
     def history(a, carry):
         scan_chunk(a)
@@ -320,7 +370,8 @@
                 pltpu.VMEM((2, LEVELS, ORBITALS, 256), F32),
                 pltpu.VMEM((2, 2, ORBITALS, 256), F32),
                 pltpu.VMEM((2, ORBITALS, 256), F32),
-                pltpu.VMEM((2, 8, 128), F32),
+                pltpu.VMEM((2, 2 * WIDE, 256), BF16),
+                pltpu.VMEM((tm - 1, 2, 8, 128), F32),
                 pltpu.VMEM((2, 2, rows, WIDE, 256), F32),
                 pltpu.VMEM((2 * rows // ROW_GROUP, 2, ROW_GROUP * WIDE, 128), F32),
                 pltpu.VMEM((chunks, 8, 128), F32),
@@ -328,7 +379,7 @@
                 pltpu.VMEM((2, 8, 128), F32),
                 pltpu.VMEM((tm, 2, 8, 128), F32),
                 dma((chunks,)), dma((chunks,)), dma((chunks,)), dma((chunks, rows // ROW_GROUP)),
-                dma((chunks,)), dma((chunks,)), dma(()), dma(()),
+                dma((chunks,)), dma((chunks,)), dma(()), dma(()), pltpu.SemaphoreType.REGULAR, pltpu.SemaphoreType.REGULAR,
             ],
             compiler_params=pltpu.CompilerParams(
                 collective_id=0, has_side_effects=True, vmem_limit_bytes=56 << 20

time: 293 us -> 291 us (level)
  Pallas kernels: 290 us -> 287 us
    pallas_call x1, Pallas kernels: 290 us -> 287 us  [shards(): pl.pallas_call(functools.partial(kernel, mom, tm, rows), out_shape=pltpu....]
where the time goes in v3:
time: 291 us; the launch traced here: 289 us
  Pallas kernels  287 us (99%)
    pallas_call x1, Pallas kernels, shards(): pl.pallas_call(functools.partial(kernel, mom, tm, rows), out_shape=pltpu....  287 us

profile of v3, /device:TPU:33, one launch (start us, length us, event | category | flops | bytes accessed | tf_op | source)
XLA Modules:
  0.0 288.6 jit_solution(2829240481650707168)
XLA Ops:
  0.0 286.6 %shard_map.64 = bf16[2,32,128,256]{3,2,1,0:T(8,128)(2,1)S(1)} custom-call(bf16[2,32,128,256]{3,2,1,0:T(8,128)(2,1)} %green.1, bf16[2,32,128,256]{3,2,1,0:T(8,128)(2,1)} %hole.1, f32[2,8,256]{2,1,0:T(8,128)} %decay.1, f32[2,8,256]{2,1,0:T(8,128)} %phase.1, bf16[128,128]{1,0:T(8,128)(2,1)} %constant.4.clone.plus, bf16[128,128]{1,0:T(8,128)(2,1)} %constant.5.clone.minus), custom_call_target="tpu_custom_call" | custom-call | tf_op jit(solution)/shard_map/pallas_call | solution.py:358
  286.6 2.0 copy.8

commit v4 on v3

--- a/solution.py
+++ b/solution.py
@@ -33,11 +33,11 @@
 
 def kernel(
     mom, tm, rows,
-    green, hole, decay, phase, plus, minus,
+    green, hole, decay_in, phase_in, plus_in, minus_in,
     out,
-    gh, sb, rb, tg, th, ts, coef, turn, grow, heavy, reach, local, wide,
+    decay, phase, plus, minus, gh, sb, rb, tg, th, ts, coef, turn, grow, heavy, reach, local, wide,
     est, ebox, pst, pbox,
-    fwd_send, fwd_recv, ret_send, ret_recv, end_send, end_recv, prod_send, prod_recv, line_z, line_x,
+    fwd_send, fwd_recv, ret_send, ret_recv, end_send, end_recv, prod_send, prod_recv, table_sem, line_z, line_x,
 ):
     m = lax.axis_index("mom")
     n = lax.axis_index("tm")
@@ -85,6 +85,14 @@
         return carry
 
     lax.fori_loop(1, tm, greet_tm, 0)
+    tables = [
+        pltpu.make_async_copy(source, kept, table_sem.at[i])
+        for i, (source, kept) in enumerate(
+            ((decay_in, decay), (phase_in, phase), (plus_in, plus), (minus_in, minus))
+        )
+    ]
+    for copy in tables:
+        copy.start()
     pl.semaphore_wait(barrier, 4 + across - 1 + tm - 1)
     for dz in (2, -2):
         greet(line_z, mom=at(0, dz))
@@ -130,6 +138,8 @@
     pl.semaphore_wait(line_x, across - 1)
     lax.fori_loop(0, chunks, send_far, 0)
 
+    for copy in tables:
+        copy.wait()
     lane = lax.broadcasted_iota(jnp.int32, (ORBITALS, 256), 1)
     sub = lax.broadcasted_iota(jnp.int32, (8, 128), 0)
     col = lax.broadcasted_iota(jnp.int32, (8, 128), 1)
@@ -358,9 +368,13 @@
         return pl.pallas_call(
             functools.partial(kernel, mom, tm, rows),
             out_shape=pltpu.VMEM(green.shape, BF16),
-            in_specs=[anywhere, anywhere, vmem, vmem, vmem, vmem],
+            in_specs=[anywhere] * 6,
             out_specs=vmem,
             scratch_shapes=[
+                pltpu.VMEM(decay_log.shape, F32),
+                pltpu.VMEM(phase_step.shape, F32),
+                pltpu.VMEM((2 * MOMENTA, 2 * MOMENTA), BF16),
+                pltpu.VMEM((2 * MOMENTA, 2 * MOMENTA), BF16),
                 pltpu.VMEM((chunks, 2 * MOMENTA, WIDE, 256), BF16),
                 pltpu.VMEM((chunks, MOMENTA, WIDE, 256), BF16),
                 pltpu.VMEM((chunks, mom, 2, WIDE, 256), BF16),
@@ -379,7 +393,7 @@
                 pltpu.VMEM((2, 8, 128), F32),
                 pltpu.VMEM((tm, 2, 8, 128), F32),
                 dma((chunks,)), dma((chunks,)), dma((chunks,)), dma((chunks, rows // ROW_GROUP)),
-                dma((chunks,)), dma((chunks,)), dma(()), dma(()), pltpu.SemaphoreType.REGULAR, pltpu.SemaphoreType.REGULAR,
+                dma((chunks,)), dma((chunks,)), dma(()), dma(()), dma((4,)), pltpu.SemaphoreType.REGULAR, pltpu.SemaphoreType.REGULAR,
             ],
             compiler_params=pltpu.CompilerParams(
                 collective_id=0, has_side_effects=True, vmem_limit_bytes=56 << 20

time: 291 us -> 290 us (level)
  no operation moved by 1% of the time
where the time goes in v4:
time: 290 us; the launch traced here: 288 us
  Pallas kernels  286 us (99%)
    pallas_call x1, Pallas kernels, shards(): pl.pallas_call(functools.partial(kernel, mom, tm, rows), out_shape=pltpu....  286 us

profile of v4, /device:TPU:33, one launch (start us, length us, event | category | flops | bytes accessed | tf_op | source)
XLA Modules:
  0.0 288.0 jit_solution(8678133416285052283)
XLA Ops:
  0.0 286.0 %shard_map.64 = bf16[2,32,128,256]{3,2,1,0:T(8,128)(2,1)S(1)} custom-call(bf16[2,32,128,256]{3,2,1,0:T(8,128)(2,1)} %green.1, bf16[2,32,128,256]{3,2,1,0:T(8,128)(2,1)} %hole.1, f32[2,8,256]{2,1,0:T(8,128)} %decay_in.1, f32[2,8,256]{2,1,0:T(8,128)} %phase_in.1, bf16[128,128]{1,0:T(8,128)(2,1)} %constant.4.clone.plus_in, bf16[128,128]{1,0:T(8,128)(2,1)} %constant.5.clone.minus_in), custom_call_target="tpu_custom_call" | custom-call | tf_op jit(solution)/shard_map/pallas_call | solution.py:368
  286.0 2.0 copy.8

commit v5 on v4

--- a/solution.py
+++ b/solution.py
@@ -49,10 +49,7 @@
     x, z = m // side, m % side
 
     def offset(j):
-        q, i = j // 8, j % 8
-        turned = i // 4
-        dz = jnp.where(q == 0, 4 * turned, (4 - q) * (1 - 2 * turned))
-        return i % 4, dz
+        return j // side, j % side
 
     def target(j):
         dx, dz = offset(j)
@@ -110,7 +107,7 @@
             ).start()
 
     def send_near(a, carry):
-        for j in (16, 20, 24, 28):
+        for j in (1, side - 1, 2, side - 2):
             send_field(a, j)
         return carry
 
@@ -123,7 +120,7 @@
             ).start()
 
         def one(j, inner):
-            @pl.when(jnp.logical_or(j < 16, j % 4 != 0))
+            @pl.when(jnp.logical_or(j >= side, jnp.logical_and(j > 2, j < side - 2)))
             def _():
                 send_field(a, j)
 

time: 290 us -> 290 us (level)
  no operation moved by 1% of the time
where the time goes in v5:
time: 290 us; the launch traced here: 288 us
  Pallas kernels  286 us (99%)
    pallas_call x1, Pallas kernels, shards(): pl.pallas_call(functools.partial(kernel, mom, tm, rows), out_shape=pltpu....  286 us

profile of v5, /device:TPU:33, one launch (start us, length us, event | category | flops | bytes accessed | tf_op | source)
XLA Modules:
  0.0 287.9 jit_solution(12462333378064334410)
XLA Ops:
  0.0 285.9 %shard_map.64 = bf16[2,32,128,256]{3,2,1,0:T(8,128)(2,1)S(1)} custom-call(bf16[2,32,128,256]{3,2,1,0:T(8,128)(2,1)} %green.1, bf16[2,32,128,256]{3,2,1,0:T(8,128)(2,1)} %hole.1, f32[2,8,256]{2,1,0:T(8,128)} %decay_in.1, f32[2,8,256]{2,1,0:T(8,128)} %phase_in.1, bf16[128,128]{1,0:T(8,128)(2,1)} %constant.4.clone.plus_in, bf16[128,128]{1,0:T(8,128)(2,1)} %constant.5.clone.minus_in), custom_call_target="tpu_custom_call" | custom-call | tf_op jit(solution)/shard_map/pallas_call | solution.py:365
  285.9 2.0 copy.8
